TPU v7x, 32 devices: a whole 2x2x4 slice. The times are simulated.
32 devices in a mesh: groups: 2 (over x), seq: 16 (over z, y, core).
Axes of the slice: x: 2, y: 2, z: 4, core: 2. Of those that a mesh axis runs over, the one named last changes fastest.
Arguments:
- tokens: bfloat16 [8192, 4096], P(('groups', 'seq')), parts along dimension 0, may hold values from -14 to 14, as said below
- norm_gain: float32 [4096], replicated, may hold values from 0.25 to 1.75
- w_query: bfloat16 [4096, 2048], P('seq'), may hold values from -1 to 1, as said below
- w_key: bfloat16 [4096, 512], P('seq'), may hold values from -24 to 24
- w_value: bfloat16 [4096, 512], P('seq'), may hold values from -0.09375 to 0.09375
- passage_blocks: int32 [64], P(('groups', 'seq')), parts along dimension 0, may hold values from 0 to 9, as said below
Outputs:
- attended: bfloat16 [8192, 2048], P(('groups', 'seq')), parts along dimension 0
There are 2 independent parts, one for each index of `groups`. A program takes and returns all parts, laid end to end along the dimension named above; an argument that names none is the same for every part. Nothing has to cross between parts.
Inputs may be any that keep to these rules, and one draw needn't show every extreme that they name: `passage_blocks`: passage numbers never fall along the row; each passage covers 1 to 7 whole blocks; the first and the last passage of the row cover exactly 7. `tokens`: hidden states of order one. `w_query`: entries of order 4096 ** -0.5.
All inputs are finite; a program needn't handle non-finite values.
Results may differ from a plain program's by a relative error of at most 0.0049.
The roundings to bfloat16 on the way count: a program that leaves them out, or rounds other values in their place, can miss the bound.
Values may be sent and summed in bfloat16 or wider, within the bound.
A program may use at most 128 MiB of HBM per device.

v0:
```python
import jax
import jax.numpy as jnp
from jax import lax
from jax.sharding import PartitionSpec as P

HD = 128
QH = 16
KVH = 4
REACH = 3


def passed_along(value, axis, by):
    peers = lax.axis_size(axis)
    pairs = [(i, i + by) for i in range(peers) if 0 <= i + by < peers]
    return lax.ppermute(value, axis, pairs)


def normalize(tokens, norm_gain):
    widened = tokens.astype(jnp.float32)
    inverse = lax.rsqrt(jnp.mean(widened * widened, axis=-1, keepdims=True) + 1e-05)
    return (widened * inverse * norm_gain).astype(jnp.bfloat16)


def dense_attention(query_heads, all_keys, all_values, query_ids, key_ids):
    row_count = query_heads.shape[1]
    key_count = all_keys.shape[0]
    key_heads = all_keys.reshape(key_count, KVH, HD).transpose(1, 0, 2)
    value_heads = all_values.reshape(key_count, KVH, HD).transpose(1, 0, 2)
    allowed = query_ids[:, None] == key_ids[None, :]

    def one_head(operands):
        head_query, head_keys, head_values = operands
        scores = jnp.einsum(
            "tgd,sd->gts", head_query, head_keys, preferred_element_type=jnp.float32
        ) * HD ** (-0.5)
        scores = jnp.where(allowed[None], scores, -1e30)
        row_max = jnp.max(scores, axis=-1, keepdims=True)
        weights = jnp.exp(scores - row_max)
        row_total = jnp.sum(weights, axis=-1)
        rounded = weights.astype(jnp.bfloat16)
        mixed = jnp.einsum("gts,sd->tgd", rounded, head_values, preferred_element_type=jnp.float32)
        return mixed / row_total.transpose(1, 0)[:, :, None]

    stacked = lax.map(one_head, (query_heads, key_heads, value_heads))
    return stacked.transpose(1, 0, 2, 3).reshape(row_count, QH * HD)


def on_device(tokens, norm_gain, w_query, w_key, w_value, passage_blocks):
    row_count = tokens.shape[0]
    block_len = row_count // passage_blocks.shape[0]
    normed = normalize(tokens, norm_gain)

    def add_rows(piece):
        return jnp.dot(normed, piece, preferred_element_type=jnp.float32)

    pieces = (
        lax.all_gather(w_query, "seq", axis=0, tiled=True),
        lax.all_gather(w_key, "seq", axis=0, tiled=True),
        lax.all_gather(w_value, "seq", axis=0, tiled=True),
    )
    query = add_rows(pieces[0])
    keys = add_rows(pieces[1])
    values = add_rows(pieces[2])
    key_rounded = keys.astype(jnp.bfloat16)
    value_rounded = values.astype(jnp.bfloat16)
    passage_ids = jnp.repeat(passage_blocks + 1, block_len).astype(jnp.bfloat16)
    own = (key_rounded, value_rounded, passage_ids)
    earlier = []
    later = []
    for distance in range(1, REACH + 1):
        for direction in (1, -1):
            moved = passed_along(
                (key_rounded, value_rounded, passage_ids), "seq", direction * distance
            )
            if direction == 1:
                earlier.insert(0, moved)
            else:
                later.append(moved)
    pieces = earlier + [own] + later
    query_rounded = query.astype(jnp.bfloat16)
    query_heads = query_rounded.reshape(row_count, KVH, QH // KVH, HD).transpose(1, 0, 2, 3)
    all_keys = jnp.concatenate([piece[0] for piece in pieces], axis=0)
    all_values = jnp.concatenate([piece[1] for piece in pieces], axis=0)
    all_ids = jnp.concatenate([piece[2] for piece in pieces], axis=0)
    result = dense_attention(query_heads, all_keys, all_values, passage_ids, all_ids)
    return result.astype(jnp.bfloat16)


def solution(mesh):
    in_specs = (
        P(("groups", "seq"), None),
        P(),
        P("seq", None),
        P("seq", None),
        P("seq", None),
        P(("groups", "seq")),
    )
    out_specs = P(("groups", "seq"), None)
    return jax.shard_map(
        on_device, mesh=mesh, in_specs=in_specs, out_specs=out_specs, check_vma=False
    )
```

profile of v0, /device:TPU:9, one launch (start us, length us, event | category | flops | bytes accessed | tf_op | source)
XLA Modules:
  0.0 310.3 jit_solution(10154052325057209868)
XLA Ops:
  9.5 3.8 %collective-permute-start.6 = (bf16[256]{0:T(256)(128)(2,1)S(1)}, bf16[256]{0:T(256)(128)(2,1)S(1)}, u32[]{:S(2)}, u32[]{:S(2)}) collective-permute-start(bf16[256]{0:T(256)(128)(2,1)S(1)} %broadcast_bitcast_fusion), channel_id=1, source_target_pairs={{0,3},{1,4},{2,5},{3,6},{4,7},{5,8},{6,9},{7,10},{8,11},{9,12},{10... | collective-permute-start | bytes 1544 | tf_op jit(solution)/shard_map/ppermute | solution.py:15
  13.2 3.1 %collective-permute-start.7 = (bf16[256]{0:T(256)(128)(2,1)S(1)}, bf16[256]{0:T(256)(128)(2,1)S(1)}, u32[]{:S(2)}, u32[]{:S(2)}) collective-permute-start(bf16[256]{0:T(256)(128)(2,1)S(1)} %broadcast_bitcast_fusion), channel_id=1, source_target_pairs={{0,2},{1,3},{2,4},{3,5},{4,6},{5,7},{6,8},{7,9},{8,10},{9,11},{10,... | collective-permute-start | bytes 1544 | tf_op jit(solution)/shard_map/ppermute | solution.py:15
  16.4 3.1 collective-permute-start.8
  21.4 3.0 collective-permute-start.10
  24.5 2.1 fusion.31
  26.6 2.4 collective-permute-start.11
  32.4 29.1 %all-gather.6.cloned.1.call-done = bf16[4096,512]{1,0:T(8,128)(2,1)} async-done(((bf16[256,512]{1,0:T(8,128)(2,1)}), bf16[4096,512]{1,0:T(8,128)(2,1)}) %all-gather.6.cloned.1.call-update) | async-done | bytes 4194320 | tf_op jit(solution)/shard_map/all_gather | solution.py:58
  61.5 3.5 %convolution_convert_fusion.1 = bf16[256,512]{1,0:T(8,128)(2,1)S(1)} fusion(bf16[4096,512]{1,0:T(8,128)(2,1)} %all-gather.6.cloned.1.call-done, bf16[256,4096]{1,0:T(8,128)(2,1)S(1)} %copy-done, f32[4096]{0:T(1024)S(1)} %copy-done.1, f32[256]{0:T(256)S(1)} %add_rsqrt_fusion), kind=kOutput, calls=%fused_computation.31 | convolution fusion | flops 1078067200 | bytes 6571008 | tf_op jit(solution)/shard_map/dot_general | solution.py:54
  65.1 2.6 collective-permute-start.12
  67.7 2.2 collective-permute-start.13
  69.9 3.5 %collective-permute-start.14 = (bf16[256,512]{1,0:T(8,128)(2,1)S(1)}, bf16[256,512]{1,0:T(8,128)(2,1)S(1)}, u32[]{:S(2)}, u32[]{:S(2)}) collective-permute-start(bf16[256,512]{1,0:T(8,128)(2,1)S(1)} %convolution_convert_fusion.1), channel_id=1, source_target_pairs={{0,1},{1,2},{2,3},{3,4},{4,5},{5,6},{6,7},{7,8},{8,9},{9,10},{10,1... | collective-permute-start | bytes 786440 | tf_op jit(solution)/shard_map/ppermute | solution.py:15
  75.4 4.0 %collective-permute-start.16 = (bf16[256,512]{1,0:T(8,128)(2,1)S(1)}, bf16[256,512]{1,0:T(8,128)(2,1)S(1)}, u32[]{:S(2)}, u32[]{:S(2)}) collective-permute-start(bf16[256,512]{1,0:T(8,128)(2,1)S(1)} %convolution_convert_fusion.1), channel_id=1, source_target_pairs={{2,0},{3,1},{4,2},{5,3},{6,4},{7,5},{8,6},{9,7},{10,8},{11,9},{12,... | collective-permute-start | bytes 786440 | tf_op jit(solution)/shard_map/ppermute | solution.py:15
  79.4 38.4 %all-gather.4.cloned.1.call-done = bf16[4096,512]{1,0:T(8,128)(2,1)} async-done(((bf16[256,512]{1,0:T(8,128)(2,1)}), bf16[4096,512]{1,0:T(8,128)(2,1)}) %all-gather.4.cloned.1.call-update) | async-done | bytes 4194320 | tf_op jit(solution)/shard_map/all_gather | solution.py:59
  117.7 3.5 %convolution_convert_fusion.2 = bf16[256,512]{1,0:T(8,128)(2,1)S(1)} fusion(bf16[4096,512]{1,0:T(8,128)(2,1)} %all-gather.4.cloned.1.call-done, bf16[256,4096]{1,0:T(8,128)(2,1)S(1)} %copy-done, f32[4096]{0:T(1024)S(1)} %copy-done.1, f32[256]{0:T(256)S(1)} %add_rsqrt_fusion), kind=kOutput, calls=%fused_computation.32 | convolution fusion | flops 1078067200 | bytes 6571008 | tf_op jit(solution)/shard_map/dot_general | solution.py:54
  121.3 2.6 collective-permute-start
  125.6 2.2 collective-permute-start.1
  128.5 3.5 %collective-permute-start.2 = (bf16[256,512]{1,0:T(8,128)(2,1)S(1)}, bf16[256,512]{1,0:T(8,128)(2,1)S(1)}, u32[]{:S(2)}, u32[]{:S(2)}) collective-permute-start(bf16[256,512]{1,0:T(8,128)(2,1)S(1)} %convolution_convert_fusion.2), channel_id=1, source_target_pairs={{0,1},{1,2},{2,3},{3,4},{4,5},{5,6},{6,7},{7,8},{8,9},{9,10},{10,1... | collective-permute-start | bytes 786440 | tf_op jit(solution)/shard_map/ppermute | solution.py:15
  133.4 2.2 collective-permute-done
  137.6 4.7 %collective-permute-done.1 = bf16[256,512]{1,0:T(8,128)(2,1)S(1)} collective-permute-done((bf16[256,512]{1,0:T(8,128)(2,1)S(1)}, bf16[256,512]{1,0:T(8,128)(2,1)S(1)}, u32[]{:S(2)}, u32[]{:S(2)}) %collective-permute-start.1) | collective-permute-done | bytes 262176 | tf_op jit(solution)/shard_map/ppermute | solution.py:15
  144.3 4.8 %collective-permute-done.2 = bf16[256,512]{1,0:T(8,128)(2,1)S(1)} collective-permute-done((bf16[256,512]{1,0:T(8,128)(2,1)S(1)}, bf16[256,512]{1,0:T(8,128)(2,1)S(1)}, u32[]{:S(2)}, u32[]{:S(2)}) %collective-permute-start.2) | collective-permute-done | bytes 262176 | tf_op jit(solution)/shard_map/ppermute | solution.py:15
  149.1 5.6 %collective-permute-start.5 = (bf16[256,512]{1,0:T(8,128)(2,1)S(1)}, bf16[256,512]{1,0:T(8,128)(2,1)S(1)}, u32[]{:S(2)}, u32[]{:S(2)}) collective-permute-start(bf16[256,512]{1,0:T(8,128)(2,1)S(1)} %convolution_convert_fusion.2), channel_id=1, source_target_pairs={{3,0},{4,1},{5,2},{6,3},{7,4},{8,5},{9,6},{10,7},{11,8},{12,9},{13... | collective-permute-start | bytes 786440 | tf_op jit(solution)/shard_map/ppermute | solution.py:15
  155.0 2.1 collective-permute-start.17
  157.7 21.9 %collective-permute-done.5 = bf16[256,512]{1,0:T(8,128)(2,1)S(1)} collective-permute-done((bf16[256,512]{1,0:T(8,128)(2,1)S(1)}, bf16[256,512]{1,0:T(8,128)(2,1)S(1)}, u32[]{:S(2)}, u32[]{:S(2)}) %collective-permute-start.5) | collective-permute-done | bytes 262176 | tf_op jit(solution)/shard_map/ppermute | solution.py:15
  179.7 2.5 copy.13
  186.2 73.5 %all-gather.8.cloned.1.call-done = bf16[4096,2048]{1,0:T(8,128)(2,1)} async-done(((bf16[256,2048]{1,0:T(8,128)(2,1)}), bf16[4096,2048]{1,0:T(8,128)(2,1)}) %all-gather.8.cloned.1.call-update) | async-done | bytes 16777232 | tf_op jit(solution)/shard_map/all_gather | solution.py:57
  259.6 11.0 %convolution_convert_fusion = bf16[256,2048]{1,0:T(8,128)(2,1)S(1)} fusion(bf16[4096,2048]{1,0:T(8,128)(2,1)} %all-gather.8.cloned.1.call-done, bf16[256,4096]{1,0:T(8,128)(2,1)} %param.8, f32[4096]{0:T(1024)S(1)} %copy-done.1, f32[256]{0:T(256)S(1)} %add_rsqrt_fusion), kind=kOutput, calls=%fused_computation.29 | convolution fusion | flops 4299685888 | bytes 19940352 | tf_op jit(solution)/shard_map/dot_general | solution.py:54
  273.6 27.9 %while.11 = (s32[]{:T(128)}, bf16[4,256,4,128]{1,3,2,0:T(8,128)(2,1)}, bf16[4,1792,128]{1,2,0:T(8,128)(2,1)}, bf16[4,1792,128]{2,1,0:T(8,128)(2,1)S(1)}, bf16[4,...) while((s32[]{:T(128)}, ...), condition=%wide.region_4.5_spmd.clone, body=%wide.region_1.4_spmd.clone.sunk | while | flops 960296960 | bytes 25585748 | solution.py:44
  276.9 3.7 %fusion.50 = bf16[4,256,4,128]{1,3,2,0:T(8,128)(2,1)} fusion(bf16[4,256,4,128]{1,3,2,0:T(8,128)(2,1)} %get-tuple-element.128, s32[]{:T(128)} %get-tuple-element.127, f32[1792,256,4]{1,0,2:T(8,128)S(1)} %get-tuple-element.117, f32[4,256]{1,0:T(4,128)S(1)} %get-tuple-element.118, pred[256,1792]{0,1:T(8,128)(4,1)S(1)} %broadcast_compare_fusion.2, ...), kind=kOutput, calls=%fused_computation.11.clone.1 | convolution fusion | flops 477233152 | bytes 8791040 | tf_op jit(solution)/shard_map/while/body/eval_jaxpr/gts,sd->tgd/dot_general | solution.py:41
  283.8 3.8 %fusion.50 = bf16[4,256,4,128]{1,3,2,0:T(8,128)(2,1)} fusion(bf16[4,256,4,128]{1,3,2,0:T(8,128)(2,1)} %get-tuple-element.128, s32[]{:T(128)} %get-tuple-element.127, f32[1792,256,4]{1,0,2:T(8,128)S(1)} %get-tuple-element.117, f32[4,256]{1,0:T(4,128)S(1)} %get-tuple-element.118, pred[256,1792]{0,1:T(8,128)(4,1)S(1)} %broadcast_compare_fusion.2, ...), kind=kOutput, calls=%fused_computation.11.clone.1 | convolution fusion | flops 477233152 | bytes 8791040 | tf_op jit(solution)/shard_map/while/body/eval_jaxpr/gts,sd->tgd/dot_general | solution.py:41
  290.8 3.8 %fusion.50 = bf16[4,256,4,128]{1,3,2,0:T(8,128)(2,1)} fusion(bf16[4,256,4,128]{1,3,2,0:T(8,128)(2,1)} %get-tuple-element.128, s32[]{:T(128)} %get-tuple-element.127, f32[1792,256,4]{1,0,2:T(8,128)S(1)} %get-tuple-element.117, f32[4,256]{1,0:T(4,128)S(1)} %get-tuple-element.118, pred[256,1792]{0,1:T(8,128)(4,1)S(1)} %broadcast_compare_fusion.2, ...), kind=kOutput, calls=%fused_computation.11.clone.1 | convolution fusion | flops 477233152 | bytes 8791040 | tf_op jit(solution)/shard_map/while/body/eval_jaxpr/gts,sd->tgd/dot_general | solution.py:41
  297.8 3.7 %fusion.50 = bf16[4,256,4,128]{1,3,2,0:T(8,128)(2,1)} fusion(bf16[4,256,4,128]{1,3,2,0:T(8,128)(2,1)} %get-tuple-element.128, s32[]{:T(128)} %get-tuple-element.127, f32[1792,256,4]{1,0,2:T(8,128)S(1)} %get-tuple-element.117, f32[4,256]{1,0:T(4,128)S(1)} %get-tuple-element.118, pred[256,1792]{0,1:T(8,128)(4,1)S(1)} %broadcast_compare_fusion.2, ...), kind=kOutput, calls=%fused_computation.11.clone.1 | convolution fusion | flops 477233152 | bytes 8791040 | tf_op jit(solution)/shard_map/while/body/eval_jaxpr/gts,sd->tgd/dot_general | solution.py:41
  301.5 2.3 copy.14
  (69 shorter events, 38.6 us)
Async XLA Ops:
  6.5 55.0 %copy-start = (bf16[256,4096]{1,0:T(8,128)(2,1)S(1)}, bf16[256,4096]{1,0:T(8,128)(2,1)}, u32[]{:S(2)}) copy-start(bf16[256,4096]{1,0:T(8,128)(2,1)} %param.8) | copy-start | bytes 6291460
  6.5 55.0 %copy-start.1 = (f32[4096]{0:T(1024)S(1)}, f32[4096]{0:T(1024)}, u32[]{:S(2)}) copy-start(f32[4096]{0:T(1024)} %param.9) | copy-start | bytes 49156
  6.5 55.0 %all-gather.6.cloned.1.call-start = ((), (), s32[]{:S(2)}) async-start(), calls=%async_computation.1 | async-start | bytes 4456448 | tf_op jit(solution)/shard_map/all_gather | solution.py:58
  7.3 110.5 %all-gather.4.cloned.1.call-start = ((), (), s32[]{:S(2)}) async-start(), calls=%async_computation | async-start | bytes 4456448 | tf_op jit(solution)/shard_map/all_gather | solution.py:59
  8.0 251.6 %all-gather.8.cloned.1.call-start = ((), (), s32[]{:S(2)}) async-start(), calls=%async_computation.2 | async-start | bytes 17825792 | tf_op jit(solution)/shard_map/all_gather | solution.py:57
  9.5 17.1 %collective-permute-start.6 = (bf16[256]{0:T(256)(128)(2,1)S(1)}, bf16[256]{0:T(256)(128)(2,1)S(1)}, u32[]{:S(2)}, u32[]{:S(2)}) collective-permute-start(bf16[256]{0:T(256)(128)(2,1)S(1)} %broadcast_bitcast_fusion), channel_id=1, source_target_pairs={{0,3},{1,4},{2,5},{3,6},{4,7},{5,8},{6,9},{7,10},{8,11},{9,12},{10... | collective-permute-start | bytes 1544 | tf_op jit(solution)/shard_map/ppermute | solution.py:15
  13.2 16.0 %collective-permute-start.7 = (bf16[256]{0:T(256)(128)(2,1)S(1)}, bf16[256]{0:T(256)(128)(2,1)S(1)}, u32[]{:S(2)}, u32[]{:S(2)}) collective-permute-start(bf16[256]{0:T(256)(128)(2,1)S(1)} %broadcast_bitcast_fusion), channel_id=1, source_target_pairs={{0,2},{1,3},{2,4},{3,5},{4,6},{5,7},{6,8},{7,9},{8,10},{9,11},{10,... | collective-permute-start | bytes 1544 | tf_op jit(solution)/shard_map/ppermute | solution.py:15
  16.4 13.1 %collective-permute-start.8 = (bf16[256]{0:T(256)(128)(2,1)S(1)}, bf16[256]{0:T(256)(128)(2,1)S(1)}, u32[]{:S(2)}, u32[]{:S(2)}) collective-permute-start(bf16[256]{0:T(256)(128)(2,1)S(1)} %broadcast_bitcast_fusion), channel_id=1, source_target_pairs={{0,1},{1,2},{2,3},{3,4},{4,5},{5,6},{6,7},{7,8},{8,9},{9,10},{10,1... | collective-permute-start | bytes 1544 | tf_op jit(solution)/shard_map/ppermute | solution.py:15
  19.5 10.4 %collective-permute-start.9 = (bf16[256]{0:T(256)(128)(2,1)S(1)}, bf16[256]{0:T(256)(128)(2,1)S(1)}, u32[]{:S(2)}, u32[]{:S(2)}) collective-permute-start(bf16[256]{0:T(256)(128)(2,1)S(1)} %broadcast_bitcast_fusion), channel_id=1, source_target_pairs={{1,0},{2,1},{3,2},{4,3},{5,4},{6,5},{7,6},{8,7},{9,8},{10,9},{11,1... | collective-permute-start | bytes 1544 | tf_op jit(solution)/shard_map/ppermute | solution.py:15
  21.4 8.7 %collective-permute-start.10 = (bf16[256]{0:T(256)(128)(2,1)S(1)}, bf16[256]{0:T(256)(128)(2,1)S(1)}, u32[]{:S(2)}, u32[]{:S(2)}) collective-permute-start(bf16[256]{0:T(256)(128)(2,1)S(1)} %broadcast_bitcast_fusion), channel_id=1, source_target_pairs={{2,0},{3,1},{4,2},{5,3},{6,4},{7,5},{8,6},{9,7},{10,8},{11,9},{12,... | collective-permute-start | bytes 1544 | tf_op jit(solution)/shard_map/ppermute | solution.py:15
  26.6 5.6 %collective-permute-start.11 = (bf16[256]{0:T(256)(128)(2,1)S(1)}, bf16[256]{0:T(256)(128)(2,1)S(1)}, u32[]{:S(2)}, u32[]{:S(2)}) collective-permute-start(bf16[256]{0:T(256)(128)(2,1)S(1)} %broadcast_bitcast_fusion), channel_id=1, source_target_pairs={{3,0},{4,1},{5,2},{6,3},{7,4},{8,5},{9,6},{10,7},{11,8},{12,9},{13... | collective-permute-start | bytes 1544 | tf_op jit(solution)/shard_map/ppermute | solution.py:15
  65.1 56.2 %collective-permute-start.12 = (bf16[256,512]{1,0:T(8,128)(2,1)S(1)}, bf16[256,512]{1,0:T(8,128)(2,1)}, u32[]{:S(2)}, u32[]{:S(2)}) collective-permute-start(bf16[256,512]{1,0:T(8,128)(2,1)S(1)} %convolution_convert_fusion.1), channel_id=1, source_target_pairs={{0,3},{1,4},{2,5},{3,6},{4,7},{5,8},{6,9},{7,10},{8,11},{9,12},{10... | collective-permute-start | bytes 786440 | tf_op jit(solution)/shard_map/ppermute | solution.py:15
  67.7 57.9 %collective-permute-start.13 = (bf16[256,512]{1,0:T(8,128)(2,1)S(1)}, bf16[256,512]{1,0:T(8,128)(2,1)S(1)}, u32[]{:S(2)}, u32[]{:S(2)}) collective-permute-start(bf16[256,512]{1,0:T(8,128)(2,1)S(1)} %convolution_convert_fusion.1), channel_id=1, source_target_pairs={{0,2},{1,3},{2,4},{3,5},{4,6},{5,7},{6,8},{7,9},{8,10},{9,11},{10,... | collective-permute-start | bytes 786440 | tf_op jit(solution)/shard_map/ppermute | solution.py:15
  69.9 58.6 %collective-permute-start.14 = (bf16[256,512]{1,0:T(8,128)(2,1)S(1)}, bf16[256,512]{1,0:T(8,128)(2,1)S(1)}, u32[]{:S(2)}, u32[]{:S(2)}) collective-permute-start(bf16[256,512]{1,0:T(8,128)(2,1)S(1)} %convolution_convert_fusion.1), channel_id=1, source_target_pairs={{0,1},{1,2},{2,3},{3,4},{4,5},{5,6},{6,7},{7,8},{8,9},{9,10},{10,1... | collective-permute-start | bytes 786440 | tf_op jit(solution)/shard_map/ppermute | solution.py:15
  73.4 108.8 %collective-permute-start.15 = (bf16[256,512]{1,0:T(8,128)(2,1)S(1)}, bf16[256,512]{1,0:T(8,128)(2,1)S(1)}, u32[]{:S(2)}, u32[]{:S(2)}) collective-permute-start(bf16[256,512]{1,0:T(8,128)(2,1)S(1)} %convolution_convert_fusion.1), channel_id=1, source_target_pairs={{1,0},{2,1},{3,2},{4,3},{5,4},{6,5},{7,6},{8,7},{9,8},{10,9},{11,1... | collective-permute-start | bytes 786440 | tf_op jit(solution)/shard_map/ppermute | solution.py:15
  75.4 107.5 %collective-permute-start.16 = (bf16[256,512]{1,0:T(8,128)(2,1)S(1)}, bf16[256,512]{1,0:T(8,128)(2,1)S(1)}, u32[]{:S(2)}, u32[]{:S(2)}) collective-permute-start(bf16[256,512]{1,0:T(8,128)(2,1)S(1)} %convolution_convert_fusion.1), channel_id=1, source_target_pairs={{2,0},{3,1},{4,2},{5,3},{6,4},{7,5},{8,6},{9,7},{10,8},{11,9},{12,... | collective-permute-start | bytes 786440 | tf_op jit(solution)/shard_map/ppermute | solution.py:15
  121.3 14.4 %collective-permute-start = (bf16[256,512]{1,0:T(8,128)(2,1)S(1)}, bf16[256,512]{1,0:T(8,128)(2,1)S(1)}, u32[]{:S(2)}, u32[]{:S(2)}) collective-permute-start(bf16[256,512]{1,0:T(8,128)(2,1)S(1)} %convolution_convert_fusion.2), channel_id=1, source_target_pairs={{0,3},{1,4},{2,5},{3,6},{4,7},{5,8},{6,9},{7,10},{8,11},{9,12},{10... | collective-permute-start | bytes 786440 | tf_op jit(solution)/shard_map/ppermute | solution.py:15
  125.6 16.7 %collective-permute-start.1 = (bf16[256,512]{1,0:T(8,128)(2,1)S(1)}, bf16[256,512]{1,0:T(8,128)(2,1)S(1)}, u32[]{:S(2)}, u32[]{:S(2)}) collective-permute-start(bf16[256,512]{1,0:T(8,128)(2,1)S(1)} %convolution_convert_fusion.2), channel_id=1, source_target_pairs={{0,2},{1,3},{2,4},{3,5},{4,6},{5,7},{6,8},{7,9},{8,10},{9,11},{10,... | collective-permute-start | bytes 786440 | tf_op jit(solution)/shard_map/ppermute | solution.py:15
  128.5 20.6 %collective-permute-start.2 = (bf16[256,512]{1,0:T(8,128)(2,1)S(1)}, bf16[256,512]{1,0:T(8,128)(2,1)S(1)}, u32[]{:S(2)}, u32[]{:S(2)}) collective-permute-start(bf16[256,512]{1,0:T(8,128)(2,1)S(1)} %convolution_convert_fusion.2), channel_id=1, source_target_pairs={{0,1},{1,2},{2,3},{3,4},{4,5},{5,6},{6,7},{7,8},{8,9},{9,10},{10,1... | collective-permute-start | bytes 786440 | tf_op jit(solution)/shard_map/ppermute | solution.py:15
  135.7 19.4 %collective-permute-start.3 = (bf16[256,512]{1,0:T(8,128)(2,1)S(1)}, bf16[256,512]{1,0:T(8,128)(2,1)S(1)}, u32[]{:S(2)}, u32[]{:S(2)}) collective-permute-start(bf16[256,512]{1,0:T(8,128)(2,1)S(1)} %convolution_convert_fusion.2), channel_id=1, source_target_pairs={{1,0},{2,1},{3,2},{4,3},{5,4},{6,5},{7,6},{8,7},{9,8},{10,9},{11,1... | collective-permute-start | bytes 786440 | tf_op jit(solution)/shard_map/ppermute | solution.py:15
  142.3 15.4 %collective-permute-start.4 = (bf16[256,512]{1,0:T(8,128)(2,1)S(1)}, bf16[256,512]{1,0:T(8,128)(2,1)S(1)}, u32[]{:S(2)}, u32[]{:S(2)}) collective-permute-start(bf16[256,512]{1,0:T(8,128)(2,1)S(1)} %convolution_convert_fusion.2), channel_id=1, source_target_pairs={{2,0},{3,1},{4,2},{5,3},{6,4},{7,5},{8,6},{9,7},{10,8},{11,9},{12,... | collective-permute-start | bytes 786440 | tf_op jit(solution)/shard_map/ppermute | solution.py:15
  149.1 30.6 %collective-permute-start.5 = (bf16[256,512]{1,0:T(8,128)(2,1)S(1)}, bf16[256,512]{1,0:T(8,128)(2,1)S(1)}, u32[]{:S(2)}, u32[]{:S(2)}) collective-permute-start(bf16[256,512]{1,0:T(8,128)(2,1)S(1)} %convolution_convert_fusion.2), channel_id=1, source_target_pairs={{3,0},{4,1},{5,2},{6,3},{7,4},{8,5},{9,6},{10,7},{11,8},{12,9},{13... | collective-permute-start | bytes 786440 | tf_op jit(solution)/shard_map/ppermute | solution.py:15
  155.0 28.6 %collective-permute-start.17 = (bf16[256,512]{1,0:T(8,128)(2,1)S(1)}, bf16[256,512]{1,0:T(8,128)(2,1)S(1)}, u32[]{:S(2)}, u32[]{:S(2)}) collective-permute-start(bf16[256,512]{1,0:T(8,128)(2,1)S(1)} %convolution_convert_fusion.1), channel_id=1, source_target_pairs={{3,0},{4,1},{5,2},{6,3},{7,4},{8,5},{9,6},{10,7},{11,8},{12,9},{13... | collective-permute-start | bytes 786440 | tf_op jit(solution)/shard_map/ppermute | solution.py:15
Sparse Core Ops, SparseCore 0:
  9.5 52.0 all-gather.5
  63.7 53.9 all-gather.3
  119.9 139.6 all-gather.7
where the time goes:
time: 314 us; the launch traced here: 310 us
  waiting for transfers between devices  179 us (57%)
  starting transfers between devices  51.5 us (16%)
  matrix products  38.2 us (12%)
  local copies, waits for them, and re-layouts  17.3 us (6%)
  between operations  13.4 us (4%)
  other arithmetic  10.4 us (3%)
    all_gather x1, waiting for transfers between devices, on_device(): lax.all_gather(w_query, 'seq', axis=0, tiled=True)  73.5 us
    ppermute x18, starting transfers between devices, passed_along(): return lax.ppermute(value, axis, pairs)  51.4 us
    all_gather x1, waiting for transfers between devices, on_device(): lax.all_gather(w_value, 'seq', axis=0, tiled=True)  38.4 us
    ppermute x18, waiting for transfers between devices, passed_along(): return lax.ppermute(value, axis, pairs)  36.4 us
    all_gather x1, waiting for transfers between devices, on_device(): lax.all_gather(w_key, 'seq', axis=0, tiled=True)  29.1 us
    dot_general x3, matrix products, add_rows(): return jnp.dot(normed, piece, preferred_element_type=jnp.float32)  18 us
    dot_general x4, matrix products, one_head(): jnp.einsum('gts,sd->tgd', rounded, head_values, preferred_element_type=jn...  15 us
    unnamed x22, local copies, waits for them, and re-layouts  6.7 us
  transfers between devices with their start and end apart: 21, of which 10 were waited for; matrix products, arithmetic and copies ran while one was open for 7% of the time, Pallas kernels for 0%

commit v1 on v0

v1 whole, which is shorter than its diff:
```python
import functools
import math

import jax
import jax.numpy as jnp
from jax import lax
from jax.experimental import pallas as pl
from jax.experimental.pallas import tpu as pltpu
from jax.sharding import PartitionSpec as P

HD = 128
QH = 16
KVH = 4
REACH = 3
GQ = QH // KVH
MESH = pl.DeviceIdType.MESH
SETS = 3
SW = 2 * HD
PIECES = 4
SLOTS = 2 * REACH + 2


def kernel(n_chips, tok_ref, gain_ref, wq_ref, wk_ref, wv_ref, id_ref, out_ref,
           xraw, xn, wkv, wq0, wq1, qbuf, win, idwin, obuf,
           send_sem, loc_sem, init_sem, zsem, ysem, hsem, tok_sem, id_sem, halo_sem, out_sem):
    nz = n_chips // 2
    rows, width = tok_ref.shape
    depth = wq_ref.shape[0]
    chunk = 2 * depth
    nblk = 2
    blk = rows // nblk
    g = lax.axis_index("groups")
    s = lax.axis_index("seq")
    gx = lax.rem(g, 2)
    gp = g + 1 - 2 * gx
    c = lax.rem(s, 2)
    p = s // 2
    y = lax.rem(p, 2)
    z = p // 2
    me4 = 2 * gx + c
    sib4 = 2 * gx + 1 - c
    xs4 = 2 * (1 - gx) + c
    xo4 = 2 * (1 - gx) + 1 - c
    zpair_right = lax.rem(z, 2) == 0

    def at_chip(q):
        return (g, 2 * q + c)

    sib = (g, 2 * p + 1 - c)
    xsame = (gp, s)
    xother = (gp, 2 * p + 1 - c)
    ypart = at_chip(p + 1 - 2 * y)
    zm, zp = at_chip(p - 2), at_chip(p + 2)
    has_zm, has_zp = z >= 1, z + 1 < nz
    zpair = at_chip(p + 2 - 4 * lax.rem(z, 2))

    sends = []
    counter = [0]

    def next_sem():
        counter[0] += 1
        return counter[0] - 1

    def guarded(cond, f):
        if cond is None:
            f()
        else:
            pl.when(cond)(f)

    def send(src, dst, rsem, dev, cond=None, idx=None):
        i = next_sem() if idx is None else idx
        d = pltpu.make_async_remote_copy(src_ref=src, dst_ref=dst, send_sem=send_sem.at[i],
                                         recv_sem=rsem, device_id=dev, device_id_type=MESH)
        guarded(cond, d.start)
        sends.append((cond, d))

    def recv(dst, rsem, dev, cond=None):
        d = pltpu.make_async_remote_copy(src_ref=dst, dst_ref=dst, send_sem=send_sem.at[0],
                                         recv_sem=rsem, device_id=dev, device_id_type=MESH)
        guarded(cond, d.wait_recv)

    def local(src, dst, i):
        d = pltpu.make_async_copy(src, dst, loc_sem.at[i])
        d.start()
        return d

    def cols(ref, head, width_, off=0):
        start = pl.multiple_of(head * (width_ if off is None else width_) + 0, HD)
        return ref.at[:, pl.ds(start, width_)]

    def qcols(head, half):
        return wq_ref.at[:, pl.ds(pl.multiple_of(head * (GQ * HD) + half * SW, HD), SW)]

    def own_rows(core):
        return pl.ds(pl.multiple_of(p * chunk + core * depth, depth), depth)

    bufs = (wkv, wq0, wq1)

    def parts(head, core):
        r = own_rows(core)
        return ((cols(wk_ref, head, HD), wkv.at[r, 0:HD]),
                (cols(wv_ref, head, HD), wkv.at[r, HD:SW]),
                (qcols(head, 0), wq0.at[r, :]),
                (qcols(head, 1), wq1.at[r, :]))

    loc_w = [local(a, b, i) for i, (a, b) in enumerate(parts(me4, c))]
    loc_x = local(tok_ref, xraw.at[me4], 4)
    loc_id = local(id_ref, idwin.at[gx, REACH + c], 5)

    def blank(lo, hi):
        def f():
            win[:, lo:hi] = jnp.zeros((2, hi - lo, rows, SW), jnp.bfloat16)
            idwin[:, lo:hi] = jnp.zeros((2, hi - lo) + id_ref.shape, jnp.int32)
        return f

    pl.when(p < 2)(blank(0, 1))
    pl.when(p < 1)(blank(1, 3))
    pl.when(p + 1 >= n_chips)(blank(5, 7))
    pl.when(p + 2 >= n_chips)(blank(7, 8))

    barrier = pltpu.get_barrier_semaphore()
    diag_up = (y == 1) & has_zp
    diag_dn = (y == 0) & has_zm
    for dev in (sib, xsame, xother, ypart):
        pl.semaphore_signal(barrier, inc=1, device_id=dev, device_id_type=MESH)
    for cond, dev in ((has_zm, zm), (has_zp, zp), (diag_up, at_chip(p + 1)), (diag_dn, at_chip(p - 1))):
        guarded(cond, functools.partial(pl.semaphore_signal, barrier, inc=1, device_id=dev, device_id_type=MESH))
    peers = sum(jnp.where(cond, 1, 0) for cond in (has_zm, has_zp, diag_up, diag_dn))
    pl.semaphore_wait(barrier, 4 + peers)

    for i, (a, b) in enumerate(parts(sib4, c)):
        send(a, b, init_sem.at[i], sib)
    prow = rows // PIECES
    for j in range(PIECES):
        r = slice(j * prow, (j + 1) * prow)
        send(tok_ref.at[r], xraw.at[me4, r], tok_sem.at[0, j], xsame)
    send(tok_ref, xraw.at[me4], tok_sem.at[2, 0], sib)
    for i, dev in enumerate((sib, xsame, xother)):
        send(id_ref, idwin.at[gx, REACH + c], id_sem.at[i], dev)

    def wchunk(buf, zz, yy, half=None):
        if half is None:
            return buf.at[pl.ds(pl.multiple_of((2 * zz + yy) * chunk, chunk), chunk)]
        return buf.at[pl.ds(pl.multiple_of((2 * zz + yy) * chunk + half * depth, depth), depth)]

    def relay(t, d):
        buf = bufs[t]
        if d == 0:
            for i in ((0, 1) if t == 0 else (t + 1,)):
                loc_w[i].wait()
                src, dst = parts(me4, 1 - c)[i]
                recv(dst, init_sem.at[i], sib)
            own = wchunk(buf, z, y)
            send(own, own, zsem.at[t, 1, 1], zm, has_zm)
            send(own, own, zsem.at[t, 0, 1], zp, has_zp)
            send(own, own, ysem.at[t, 0, 0], ypart)
            return
        left = wchunk(buf, z - d, y)
        right = wchunk(buf, z + d, y)
        has_l, has_r = z >= d, z + d < nz
        recv(right, zsem.at[t, 1, d], zp, has_r)
        if d + 1 < nz:
            send(right, right, zsem.at[t, 1, d + 1], zm, has_r & has_zm)
        recv(left, zsem.at[t, 0, d], zm, has_l)
        if d + 1 < nz:
            send(left, left, zsem.at[t, 0, d + 1], zp, has_l & has_zp)
        if d == 1:
            i, k = next_sem(), next_sem()
            rh, lh = wchunk(buf, z + 1, y, 0), wchunk(buf, z - 1, y, 0)
            odd = lax.rem(z, 2) == 1
            send(rh, rh, ysem.at[t, 1, 1], ypart, zpair_right, i)
            send(right, right, ysem.at[t, 1, 1], ypart, odd & has_r, i)
            send(lh, lh, ysem.at[t, 0, 1], ypart, odd, k)
            send(left, left, ysem.at[t, 0, 1], ypart, zpair_right & has_l, k)
            mate = wchunk(buf, z, 1 - y)
            recv(mate, ysem.at[t, 0, 0], ypart)
            mh = wchunk(buf, z, 1 - y, 1)
            send(mh, mh, hsem.at[t], zpair)
        else:
            send(right, right, ysem.at[t, 1, d], ypart, has_r)
            send(left, left, ysem.at[t, 0, d], ypart, has_l)

    def finish(t):
        buf = bufs[t]
        odd = lax.rem(z, 2) == 1
        for d in range(1, nz):
            right, left = wchunk(buf, z + d, 1 - y), wchunk(buf, z - d, 1 - y)
            has_l, has_r = z >= d, z + d < nz
            if d == 1:
                recv(wchunk(buf, z + 1, 1 - y, 0), ysem.at[t, 1, 1], ypart, zpair_right)
                recv(right, ysem.at[t, 1, 1], ypart, odd & has_r)
                recv(wchunk(buf, z - 1, 1 - y, 0), ysem.at[t, 0, 1], ypart, odd)
                recv(left, ysem.at[t, 0, 1], ypart, zpair_right & has_l)
            else:
                recv(right, ysem.at[t, 1, d], ypart, has_r)
                recv(left, ysem.at[t, 0, d], ypart, has_l)
        mh = wchunk(buf, z + 1 - 2 * lax.rem(z, 2), 1 - y, 1)
        recv(mh, hsem.at[t], zpair)

    def normalize(slot):
        step = 16

        def body(i, _):
            r = pl.ds(pl.multiple_of(i * step, step), step)
            wide = xraw[slot, r, :].astype(jnp.float32)
            inv = lax.rsqrt(jnp.mean(wide * wide, axis=-1, keepdims=True) + 1e-05)
            xn[slot, r, :] = (wide * inv * gain_ref[...]).astype(jnp.bfloat16)
            return 0

        lax.fori_loop(0, rows // step, body, 0)

    def forward_tokens(j):
        r = slice(j * prow, (j + 1) * prow)
        recv(xraw.at[xs4, r], tok_sem.at[0, j], xsame)
        send(xraw.at[xs4, r], xraw.at[xs4, r], tok_sem.at[1, j], sib)

    def project_kv(gi):
        def body(ci, _):
            r = jnp.dot(xn[2 * gi + ci], wkv[...], preferred_element_type=jnp.float32)
            win[gi, REACH + ci] = r.astype(jnp.bfloat16)
            return 0

        lax.fori_loop(0, 2, body, 0)

    def project_q(t):
        buf = bufs[t]

        def body(i, _):
            r = jnp.dot(xn[i], buf[...], preferred_element_type=jnp.float32).astype(jnp.bfloat16)
            qbuf[2 * (t - 1), i] = r[:, 0:HD]
            qbuf[2 * (t - 1) + 1, i] = r[:, HD:SW]
            return 0

        lax.fori_loop(0, 4, body, 0)

    up1, dn1, up2, dn2 = p + 1 < n_chips, p >= 1, p + 2 < n_chips, p >= 2
    routes = ((up1, p + 1, (3, 5), (1, 3)), (dn1, p - 1, (3, 5), (5, 7)),
              (up2, p + 2, (4, 5), (0, 1)), (dn2, p - 2, (3, 4), (7, 8)))
    back = ((dn1, p - 1), (up1, p + 1), (dn2, p - 2), (up2, p + 2))

    def halo_send(gi, which):
        for i, (cond, q, a, b) in enumerate(routes):
            send(win.at[gi, a[0]:a[1]], win.at[gi, b[0]:b[1]], halo_sem.at[which, i], at_chip(q), cond)

    def halo_recv(gi, which):
        for i, (_, _, a, b) in enumerate(routes):
            cond, q = back[i]
            recv(win.at[gi, b[0]:b[1]], halo_sem.at[which, i], at_chip(q), cond)

    def ids_send():
        loc_id.wait()
        recv(idwin.at[gx, REACH + 1 - c], id_sem.at[0], sib)
        recv(idwin.at[1 - gx, REACH + c], id_sem.at[1], xsame)
        recv(idwin.at[1 - gx, REACH + 1 - c], id_sem.at[2], xother)
        for i, (cond, q, a, b) in enumerate(routes):
            send(idwin.at[:, a[0]:a[1]], idwin.at[:, b[0]:b[1]], id_sem.at[3 + i], at_chip(q), cond)

    def ids_recv():
        for i, (_, _, a, b) in enumerate(routes):
            cond, q = back[i]
            recv(idwin.at[:, b[0]:b[1]], id_sem.at[3 + i], at_chip(q), cond)

    rate = HD ** (-0.5) * math.log2(math.e)
    span = 2 * REACH + 1

    def attend(gi, ci, t):
        slot = 2 * gi + ci
        key_ids = jnp.concatenate([idwin[gi, ci + j, 0:1, :] for j in range(span)], axis=1)
        for qb in range(nblk):
            mine = idwin[gi, REACH + ci, 0:1, qb * blk:qb * blk + HD]
            allowed = key_ids == jnp.concatenate([mine] * (span * rows // HD), axis=1)
            rr = slice(qb * blk, (qb + 1) * blk)

            def head(hh, _):
                q = qbuf[2 * t + hh, slot, rr, :]
                k = win[gi, pl.ds(ci, span), :, 0:HD].reshape(span * rows, HD)
                v = win[gi, pl.ds(ci, span), :, HD:SW].reshape(span * rows, HD)
                sc = lax.dot_general(q, k, (((1,), (1,)), ((), ())), preferred_element_type=jnp.float32)
                sc = jnp.where(allowed, sc, -1e30)
                top = jnp.max(sc, axis=-1, keepdims=True)
                w = jnp.exp2((sc - top) * rate)
                total = jnp.sum(w, axis=-1, keepdims=True)
                mixed = jnp.dot(w.astype(jnp.bfloat16), v, preferred_element_type=jnp.float32)
                obuf[t, slot, rr, pl.ds(pl.multiple_of(hh * HD, HD), HD)] = (mixed / total).astype(jnp.bfloat16)
                return 0

            lax.fori_loop(0, 2, head, 0)

    def out_cols(head, t):
        return out_ref.at[:, pl.ds(pl.multiple_of(head * (GQ * HD) + t * SW, HD), SW)]

    out_local = []

    def attend_set(t):
        for i, (gi, ci, dev) in enumerate(((1 - gx, 1 - c, xother), (1 - gx, c, xsame), (gx, 1 - c, sib), (gx, c, None))):
            attend(gi, ci, t)
            src = obuf.at[t, 2 * gi + ci]
            if dev is None:
                out_local.append(local(src, out_cols(me4, t), 6 + t))
            else:
                send(src, out_cols(me4, t), out_sem.at[t, i], dev)

    relay(0, 0)
    loc_x.wait()
    normalize(me4)
    relay(1, 0)
    relay(0, 1)
    ids_send()
    recv(xraw.at[sib4], tok_sem.at[2, 0], sib)
    normalize(sib4)
    last = nz - 1 + SETS - 1
    for w in range(2, last + 1):
        for t in range(SETS):
            d = w - t
            if 0 <= d < nz:
                relay(t, d)
        if w == 2:
            forward_tokens(0)
        if w == 3:
            forward_tokens(1)
            forward_tokens(2)
        if w == last - 1:
            finish(0)
            project_kv(gx)
            halo_send(gx, 0)
    forward_tokens(3)
    for j in range(PIECES):
        r = slice(j * prow, (j + 1) * prow)
        recv(xraw.at[xo4, r], tok_sem.at[1, j], sib)
    normalize(xs4)
    normalize(xo4)
    project_kv(1 - gx)
    halo_send(1 - gx, 1)
    finish(1)
    project_q(1)
    ids_recv()
    halo_recv(gx, 0)
    halo_recv(1 - gx, 1)
    attend_set(0)
    finish(2)
    project_q(2)
    attend_set(1)
    for t in range(2):
        for i, (dev, head) in enumerate(((xother, xo4), (xsame, xs4), (sib, sib4))):
            recv(out_cols(head, t), out_sem.at[t, i], dev)
    for d in out_local:
        d.wait()
    for cond, d in sends:
        guarded(cond, d.wait_send)


def solution(mesh):
    n_seq = mesh.shape["seq"]
    n_chips = n_seq // 2
    nz = n_chips // 2

    def on_device(tokens, norm_gain, w_query, w_key, w_value, passage_blocks):
        rows, width = tokens.shape
        ids = jnp.repeat(passage_blocks + 1, rows // passage_blocks.shape[0])
        ids = jnp.broadcast_to(ids[None, :], (8, rows))
        anywhere = pl.BlockSpec(memory_space=pl.ANY)
        vmem = pl.BlockSpec(memory_space=pltpu.VMEM)
        n_send = SETS * (4 * nz) + 4 + 2 * PIECES + 1 + 3 + 8 + 4 + 6 + 8
        bf = jnp.bfloat16
        dma = pltpu.SemaphoreType.DMA
        return pl.pallas_call(
            functools.partial(kernel, n_chips),
            out_shape=jax.ShapeDtypeStruct((rows, QH * HD), bf),
            in_specs=[anywhere, vmem, anywhere, anywhere, anywhere, anywhere],
            out_specs=anywhere,
            scratch_shapes=[
                pltpu.VMEM((4, rows, width), bf),
                pltpu.VMEM((4, rows, width), bf),
                pltpu.VMEM((width, SW), bf),
                pltpu.VMEM((width, SW), bf),
                pltpu.VMEM((width, SW), bf),
                pltpu.VMEM((GQ, 4, rows, HD), bf),
                pltpu.VMEM((2, SLOTS, rows, SW), bf),
                pltpu.VMEM((2, SLOTS, 8, rows), jnp.int32),
                pltpu.VMEM((2, 4, rows, SW), bf),
                dma((n_send,)), dma((8,)), dma((4,)), dma((SETS, 2, nz)), dma((SETS, 2, nz)),
                dma((SETS,)), dma((3, PIECES)), dma((7,)), dma((2, 4)), dma((2, 3)),
            ],
            compiler_params=pltpu.CompilerParams(
                collective_id=0, has_side_effects=True, vmem_limit_bytes=60 * 2**20),
        )(tokens, norm_gain[None, :], w_query, w_key, w_value, ids)

    in_specs = (
        P(("groups", "seq"), None),
        P(),
        P("seq", None),
        P("seq", None),
        P("seq", None),
        P(("groups", "seq")),
    )
    out_specs = P(("groups", "seq"), None)
    return jax.shard_map(on_device, mesh=mesh, in_specs=in_specs, out_specs=out_specs, check_vma=False)
```

time: 314 us -> 154 us (0.49)
  the two profiles are of different devices: /device:TPU:9 before, /device:TPU:26 now
where the time goes in v1:
time: 154 us
  Pallas kernels  150 us (97%)
  local copies, waits for them, and re-layouts  2.98 us (2%)
    pallas_call x1, Pallas kernels, on_device(): pl.pallas_call(functools.partial(kernel, n_chips), out_shape=jax.ShapeDty...  150 us

profile of v1, /device:TPU:26, one launch (start us, length us, event | category | flops | bytes accessed | tf_op | source)
XLA Modules:
  0.0 153.7 jit_solution(940705179131084318)
XLA Ops:
  0.0 0.7 broadcast_add_fusion
  0.7 0.1 broadcast_bitcast_fusion
  0.7 0.6 broadcast_in_dim.16.id_ref
  1.3 150.1 %shard_map.64 = bf16[256,2048]{1,0:T(8,128)(2,1)} custom-call(bf16[256,4096]{1,0:T(8,128)(2,1)} %tok_ref.1, f32[1,4096]{1,0:T(1,128)} %bitcast.3, bf16[256,2048]{1,0:T(8,128)(2,1)} %wq_ref.1, bf16[256,512]{1,0:T(8,128)(2,1)} %wk_ref.1, bf16[256,512]{1,0:T(8,128)(2,1)} %wv_ref.1, s32[8,256]{1,0:T(8,128)} %broadcast_in_dim.16.id_ref), custom_call_target="tpu_custom_call" | custom-call | tf_op jit(solution)/shard_map/pallas_call | solution.py:366
  151.4 2.3 %copy.8 = bf16[256,2048]{1,0:T(8,128)(2,1)} copy(bf16[256,2048]{1,0:T(8,128)(2,1)} %shard_map.64) | data formatting | bytes 2097152

commit v2 on v1

v2 whole, which is shorter than its diff:
```python
import functools
import math

import jax
import jax.numpy as jnp
from jax import lax
from jax.experimental import pallas as pl
from jax.experimental.pallas import tpu as pltpu
from jax.sharding import PartitionSpec as P

HD = 128
QH = 16
KVH = 4
REACH = 3
GQ = QH // KVH
MESH = pl.DeviceIdType.MESH
SETS = 3
SW = 2 * HD
PIECES = 4
SLOTS = 2 * REACH + 4


def kernel(n_chips, tok_ref, gain_ref, wq_ref, wk_ref, wv_ref, id_ref, out_ref,
           xraw, xn, wkv, wq0, wq1, qbuf, win, idwin, obuf,
           send_sem, loc_sem, init_sem, zsem, xsem, tok_sem, id_sem, halo_sem, out_sem):
    nz = n_chips // 2
    rows, width = tok_ref.shape
    nblk = 2
    blk = rows // nblk
    g = lax.axis_index("groups")
    s = lax.axis_index("seq")
    gx = lax.rem(g, 2)
    gp = g + 1 - 2 * gx
    c = lax.rem(s, 2)
    p = s // 2
    y = lax.rem(p, 2)
    z = p // 2
    me4 = 2 * y + c
    sib4 = 2 * y + 1 - c
    ys4 = 2 * (1 - y) + c
    yo4 = 2 * (1 - y) + 1 - c

    sib = (g, 4 * z + sib4)
    ysame = (g, 4 * z + ys4)
    yother = (g, 4 * z + yo4)
    twin = (gp, s)
    zm, zp = (g, s - 4), (g, s + 4)
    has_zm, has_zp = z >= 1, z + 1 < nz

    sends = []
    counter = [0]

    def guarded(cond, f):
        if cond is None:
            f()
        else:
            pl.when(cond)(f)

    def send(src, dst, rsem, dev, cond=None):
        d = pltpu.make_async_remote_copy(src_ref=src, dst_ref=dst, send_sem=send_sem.at[counter[0]],
                                         recv_sem=rsem, device_id=dev, device_id_type=MESH)
        counter[0] += 1
        guarded(cond, d.start)
        sends.append((cond, d))

    def recv(dst, rsem, dev, cond=None):
        d = pltpu.make_async_remote_copy(src_ref=dst, dst_ref=dst, send_sem=send_sem.at[0],
                                         recv_sem=rsem, device_id=dev, device_id_type=MESH)
        guarded(cond, d.wait_recv)

    def local(src, dst, i):
        d = pltpu.make_async_copy(src, dst, loc_sem.at[i])
        d.start()
        return d

    bufs = (wkv, wq0, wq1)

    def columns(head, i):
        if i < 2:
            return pl.ds(pl.multiple_of(head * HD, HD), HD)
        return pl.ds(pl.multiple_of(head * (GQ * HD) + (i - 2) * SW, HD), SW)

    weights = (wk_ref, wv_ref, wq_ref, wq_ref)
    places = ((wkv, slice(0, HD)), (wkv, slice(HD, SW)), (wq0, slice(0, SW)), (wq1, slice(0, SW)))

    def full_part(i, head, yy, cc):
        buf, lanes = places[i]
        return weights[i].at[:, :, columns(head, i)], buf.at[z, yy, cc, :, :, lanes]

    def half_part(i, head, yy, cc):
        buf, lanes = places[i]
        return weights[i].at[gx, :, columns(head, i)], buf.at[z, yy, cc, gx, :, lanes]

    loc_w = [local(*full_part(i, me4, y, c), i) for i in range(4)]
    loc_x = local(tok_ref, xraw.at[me4], 4)
    loc_id = local(id_ref, idwin.at[REACH + me4], 5)

    def blank(lo):
        def f():
            win[lo:lo + REACH] = jnp.zeros((REACH, rows, SW), jnp.bfloat16)
            idwin[lo:lo + REACH] = jnp.zeros((REACH,) + id_ref.shape, jnp.int32)
        return f

    pl.when(z < 1)(blank(0))
    pl.when(z + 1 >= nz)(blank(REACH + 4))

    barrier = pltpu.get_barrier_semaphore()
    for dev in (sib, ysame, yother, twin):
        pl.semaphore_signal(barrier, inc=1, device_id=dev, device_id_type=MESH)
    for cond, dev in ((has_zm, zm), (has_zp, zp)):
        guarded(cond, functools.partial(pl.semaphore_signal, barrier, inc=1, device_id=dev, device_id_type=MESH))
    pl.semaphore_wait(barrier, 4 + jnp.where(has_zm, 1, 0) + jnp.where(has_zp, 1, 0))

    prow = rows // PIECES
    for i in range(4):
        for k, (dev, head) in enumerate(((ysame, ys4), (yother, yo4))):
            a, b = half_part(i, head, y, c)
            send(a, b, init_sem.at[i, 1 + k], dev)
        a, b = full_part(i, sib4, y, c)
        send(a, b, init_sem.at[i, 0], sib)
    for i, dev in enumerate((sib, ysame, yother)):
        send(id_ref, idwin.at[REACH + me4], id_sem.at[i], dev)
    for j in range(PIECES):
        r = slice(j * prow, (j + 1) * prow)
        send(tok_ref.at[r], xraw.at[me4, r], tok_sem.at[0, j], ysame)
    send(tok_ref, xraw.at[me4], tok_sem.at[2, 0], sib)

    def relay(t, d):
        buf = bufs[t]
        if d == 0:
            for i in ((0, 1) if t == 0 else (t + 1,)):
                loc_w[i].wait()
                recv(full_part(i, me4, y, 1 - c)[1], init_sem.at[i, 0], sib)
                recv(half_part(i, me4, 1 - y, c)[1], init_sem.at[i, 1], ysame)
                recv(half_part(i, me4, 1 - y, 1 - c)[1], init_sem.at[i, 2], yother)
            own = buf.at[z, :, :, gx]
            send(own, own, zsem.at[t, 1, 1], zm, has_zm)
            send(own, own, zsem.at[t, 0, 1], zp, has_zp)
            mate = buf.at[z, 1 - y, :, gx]
            send(mate, mate, xsem.at[t, 0, 0], twin)
            return
        left = buf.at[z - d, :, :, gx]
        right = buf.at[z + d, :, :, gx]
        has_l, has_r = z >= d, z + d < nz
        recv(right, zsem.at[t, 1, d], zp, has_r)
        if d + 1 < nz:
            send(right, right, zsem.at[t, 1, d + 1], zm, has_r & has_zm)
        recv(left, zsem.at[t, 0, d], zm, has_l)
        if d + 1 < nz:
            send(left, left, zsem.at[t, 0, d + 1], zp, has_l & has_zp)
        send(right, right, xsem.at[t, 1, d], twin, has_r)
        send(left, left, xsem.at[t, 0, d], twin, has_l)

    def finish(t):
        buf = bufs[t]
        recv(buf.at[z, 1 - y, :, 1 - gx], xsem.at[t, 0, 0], twin)
        for d in range(1, nz):
            recv(buf.at[z + d, :, :, 1 - gx], xsem.at[t, 1, d], twin, z + d < nz)
            recv(buf.at[z - d, :, :, 1 - gx], xsem.at[t, 0, d], twin, z >= d)

    def normalize(slot):
        step = 16

        def body(i, _):
            r = pl.ds(pl.multiple_of(i * step, step), step)
            wide = xraw[slot, r, :].astype(jnp.float32)
            inv = lax.rsqrt(jnp.mean(wide * wide, axis=-1, keepdims=True) + 1e-05)
            xn[slot, r, :] = (wide * inv * gain_ref[...]).astype(jnp.bfloat16)
            return 0

        lax.fori_loop(0, rows // step, body, 0)

    def forward_tokens(j):
        r = slice(j * prow, (j + 1) * prow)
        recv(xraw.at[ys4, r], tok_sem.at[0, j], ysame)
        send(xraw.at[ys4, r], xraw.at[ys4, r], tok_sem.at[1, j], sib)

    def project_kv(yy):
        def body(ci, _):
            r = jnp.dot(xn[2 * yy + ci], wkv[...].reshape(width, SW), preferred_element_type=jnp.float32)
            win[REACH + 2 * yy + ci] = r.astype(jnp.bfloat16)
            return 0

        lax.fori_loop(0, 2, body, 0)

    def project_q(t):
        buf = bufs[t]

        def body(i, _):
            r = jnp.dot(xn[i], buf[...].reshape(width, SW), preferred_element_type=jnp.float32).astype(jnp.bfloat16)
            qbuf[2 * (t - 1), i] = r[:, 0:HD]
            qbuf[2 * (t - 1) + 1, i] = r[:, HD:SW]
            return 0

        lax.fori_loop(0, 4, body, 0)

    def halo_send(yy, which):
        for slot in range(4):
            mine = (slot // 2) == yy
            a = win.at[REACH + slot]
            if slot > 0:
                send(a, win.at[slot - 1], halo_sem.at[0, slot - 1], zp, mine & has_zp)
            if slot < 3:
                send(a, win.at[REACH + 4 + slot], halo_sem.at[1, slot], zm, mine & has_zm)

    def halo_recv():
        for j in range(REACH):
            recv(win.at[j], halo_sem.at[0, j], zm, has_zm)
            recv(win.at[REACH + 4 + j], halo_sem.at[1, j], zp, has_zp)

    def ids_send():
        loc_id.wait()
        for i, (slot, dev) in enumerate(((sib4, sib), (ys4, ysame), (yo4, yother))):
            recv(idwin.at[REACH + slot], id_sem.at[i], dev)
        send(idwin.at[4:7], idwin.at[0:3], id_sem.at[3], zp, has_zp)
        send(idwin.at[3:6], idwin.at[7:10], id_sem.at[4], zm, has_zm)

    def ids_recv():
        recv(idwin.at[0:3], id_sem.at[3], zm, has_zm)
        recv(idwin.at[7:10], id_sem.at[4], zp, has_zp)

    rate = HD ** (-0.5) * math.log2(math.e)
    span = 2 * REACH + 1

    def attend(slot, t):
        key_ids = jnp.concatenate([idwin[slot + j, 0:1, :] for j in range(span)], axis=1)
        for qb in range(nblk):
            mine = idwin[REACH + slot, 0:1, qb * blk:qb * blk + HD]
            allowed = key_ids == jnp.concatenate([mine] * (span * rows // HD), axis=1)
            rr = slice(qb * blk, (qb + 1) * blk)

            def head(hh, _):
                q = qbuf[2 * t + hh, slot, rr, :]
                k = win[pl.ds(slot, span), :, 0:HD].reshape(span * rows, HD)
                v = win[pl.ds(slot, span), :, HD:SW].reshape(span * rows, HD)
                sc = lax.dot_general(q, k, (((1,), (1,)), ((), ())), preferred_element_type=jnp.float32)
                sc = jnp.where(allowed, sc, -1e30)
                top = jnp.max(sc, axis=-1, keepdims=True)
                w = jnp.exp2((sc - top) * rate)
                total = jnp.sum(w, axis=-1, keepdims=True)
                mixed = jnp.dot(w.astype(jnp.bfloat16), v, preferred_element_type=jnp.float32)
                obuf[t, slot, rr, pl.ds(pl.multiple_of(hh * HD, HD), HD)] = (mixed / total).astype(jnp.bfloat16)
                return 0

            lax.fori_loop(0, 2, head, 0)

    def out_cols(head, t):
        return out_ref.at[:, pl.ds(pl.multiple_of(head * (GQ * HD) + t * SW, HD), SW)]

    out_local = []

    def attend_set(t):
        for i, (slot, dev) in enumerate(((yo4, yother), (ys4, ysame), (sib4, sib), (me4, None))):
            attend(slot, t)
            src = obuf.at[t, slot]
            if dev is None:
                out_local.append(local(src, out_cols(me4, t), 6 + t))
            else:
                send(src, out_cols(me4, t), out_sem.at[t, i], dev)

    relay(0, 0)
    loc_x.wait()
    normalize(me4)
    relay(1, 0)
    relay(0, 1)
    ids_send()
    recv(xraw.at[sib4], tok_sem.at[2, 0], sib)
    normalize(sib4)
    last = nz - 1 + SETS - 1
    for w in range(2, last + 1):
        for t in range(SETS):
            d = w - t
            if 0 <= d < nz:
                relay(t, d)
        if w == last - 2:
            forward_tokens(0)
        if w == last - 1:
            forward_tokens(1)
            finish(0)
            project_kv(y)
            halo_send(y, 0)
    for j in range(2, PIECES):
        forward_tokens(j)
    for j in range(PIECES):
        r = slice(j * prow, (j + 1) * prow)
        recv(xraw.at[yo4, r], tok_sem.at[1, j], sib)
    normalize(ys4)
    normalize(yo4)
    project_kv(1 - y)
    halo_send(1 - y, 1)
    finish(1)
    project_q(1)
    ids_recv()
    halo_recv()
    attend_set(0)
    finish(2)
    project_q(2)
    attend_set(1)
    for t in range(2):
        for i, (dev, head) in enumerate(((yother, yo4), (ysame, ys4), (sib, sib4))):
            recv(out_cols(head, t), out_sem.at[t, i], dev)
    for d in out_local:
        d.wait()
    for cond, d in sends:
        guarded(cond, d.wait_send)


def solution(mesh):
    n_seq = mesh.shape["seq"]
    n_chips = n_seq // 2
    nz = n_chips // 2

    def on_device(tokens, norm_gain, w_query, w_key, w_value, passage_blocks):
        rows, width = tokens.shape
        ids = jnp.repeat(passage_blocks + 1, rows // passage_blocks.shape[0])
        ids = jnp.broadcast_to(ids[None, :], (8, rows))
        anywhere = pl.BlockSpec(memory_space=pl.ANY)
        vmem = pl.BlockSpec(memory_space=pltpu.VMEM)
        n_send = SETS * (4 * nz) + 12 + 3 + 2 * PIECES + 1 + 2 + 12 + 6 + 2
        bf = jnp.bfloat16
        dma = pltpu.SemaphoreType.DMA
        half = w_query.shape[0] // 2
        weight = pltpu.VMEM((nz, 2, 2, 2, half, SW), bf)
        halves = [w.reshape(2, half, w.shape[1]) for w in (w_query, w_key, w_value)]
        return pl.pallas_call(
            functools.partial(kernel, n_chips),
            out_shape=jax.ShapeDtypeStruct((rows, QH * HD), bf),
            in_specs=[anywhere, vmem, anywhere, anywhere, anywhere, anywhere],
            out_specs=anywhere,
            scratch_shapes=[
                pltpu.VMEM((4, rows, width), bf),
                pltpu.VMEM((4, rows, width), bf),
                weight, weight, weight,
                pltpu.VMEM((GQ, 4, rows, HD), bf),
                pltpu.VMEM((SLOTS, rows, SW), bf),
                pltpu.VMEM((SLOTS, 8, rows), jnp.int32),
                pltpu.VMEM((2, 4, rows, SW), bf),
                dma((n_send,)), dma((8,)), dma((4, 3)), dma((SETS, 2, nz)), dma((SETS, 2, nz)),
                dma((3, PIECES)), dma((5,)), dma((2, REACH)), dma((2, 3)),
            ],
            compiler_params=pltpu.CompilerParams(
                collective_id=0, has_side_effects=True, vmem_limit_bytes=60 * 2**20),
        )(tokens, norm_gain[None, :], *halves, ids)

    in_specs = (
        P(("groups", "seq"), None),
        P(),
        P("seq", None),
        P("seq", None),
        P("seq", None),
        P(("groups", "seq")),
    )
    out_specs = P(("groups", "seq"), None)
    return jax.shard_map(on_device, mesh=mesh, in_specs=in_specs, out_specs=out_specs, check_vma=False)
```

time: 154 us -> 112 us (0.73)
  the two profiles are of different devices: /device:TPU:26 before, /device:TPU:9 now
where the time goes in v2:
time: 112 us
  Pallas kernels  108 us (96%)
  local copies, waits for them, and re-layouts  2.98 us (3%)
    pallas_call x1, Pallas kernels, on_device(): pl.pallas_call(functools.partial(kernel, n_chips), out_shape=jax.ShapeDty...  108 us
    unnamed x1, local copies, waits for them, and re-layouts  2.3 us

profile of v2, /device:TPU:9, one launch (start us, length us, event | category | flops | bytes accessed | tf_op | source)
XLA Modules:
  0.0 112.0 jit_solution(16824976050155695993)
XLA Ops:
  0.0 0.7 broadcast_add_fusion
  0.7 0.1 broadcast_bitcast_fusion
  0.7 0.6 broadcast_in_dim.16.id_ref
  1.3 108.4 %shard_map.64 = bf16[256,2048]{1,0:T(8,128)(2,1)} custom-call(bf16[256,4096]{1,0:T(8,128)(2,1)} %tok_ref.1, f32[1,4096]{1,0:T(1,128)} %bitcast.9, bf16[2,128,2048]{2,1,0:T(8,128)(2,1)} %bitcast.6, bf16[2,128,512]{2,1,0:T(8,128)(2,1)} %bitcast.7, bf16[2,128,512]{2,1,0:T(8,128)(2,1)} %bitcast.8, s32[8,256]{1,0:T(8,128)} %broadcast_in_dim.16.id_ref), custom_call_target="tpu_custom_call" | custom-call | tf_op jit(solution)/shard_map/pallas_call | solution.py:325
  109.7 2.3 %copy.8 = bf16[256,2048]{1,0:T(8,128)(2,1)} copy(bf16[256,2048]{1,0:T(8,128)(2,1)} %shard_map.64) | data formatting | bytes 2097152

commit v3 on v2

--- a/solution.py
+++ b/solution.py
@@ -14,7 +14,7 @@
 REACH = 3
 GQ = QH // KVH
 MESH = pl.DeviceIdType.MESH
-SETS = 3
+SETS = 2 + GQ
 SW = 2 * HD
 PIECES = 4
 SLOTS = 2 * REACH + 4
@@ -76,12 +76,18 @@
     bufs = (wkv, wq0, wq1)
 
     def columns(head, i):
-        if i < 2:
-            return pl.ds(pl.multiple_of(head * HD, HD), HD)
-        return pl.ds(pl.multiple_of(head * (GQ * HD) + (i - 2) * SW, HD), SW)
-
-    weights = (wk_ref, wv_ref, wq_ref, wq_ref)
-    places = ((wkv, slice(0, HD)), (wkv, slice(HD, SW)), (wq0, slice(0, SW)), (wq1, slice(0, SW)))
+        return pl.ds(pl.multiple_of(head * HD if i < 2 else head * (GQ * HD) + (i - 2) * HD, HD), HD)
+
+    weights = (wk_ref, wv_ref) + (wq_ref,) * GQ
+    places = tuple((bufs[i // 2], slice(i % 2 * HD, i % 2 * HD + HD)) for i in range(SETS))
+
+    def unit(t, zz, half):
+        buf, lanes = places[t]
+        return buf.at[zz, :, :, half, :, lanes]
+
+    def mates(t, half):
+        buf, lanes = places[t]
+        return buf.at[z, 1 - y, :, half, :, lanes]
 
     def full_part(i, head, yy, cc):
         buf, lanes = places[i]
@@ -91,9 +97,9 @@
         buf, lanes = places[i]
         return weights[i].at[gx, :, columns(head, i)], buf.at[z, yy, cc, gx, :, lanes]
 
-    loc_w = [local(*full_part(i, me4, y, c), i) for i in range(4)]
-    loc_x = local(tok_ref, xraw.at[me4], 4)
-    loc_id = local(id_ref, idwin.at[REACH + me4], 5)
+    loc_w = [local(*full_part(i, me4, y, c), i) for i in range(SETS)]
+    loc_x = local(tok_ref, xraw.at[me4], SETS)
+    loc_id = local(id_ref, idwin.at[REACH + me4], SETS + 1)
 
     def blank(lo):
         def f():
@@ -112,7 +118,7 @@
     pl.semaphore_wait(barrier, 4 + jnp.where(has_zm, 1, 0) + jnp.where(has_zp, 1, 0))
 
     prow = rows // PIECES
-    for i in range(4):
+    for i in range(SETS):
         for k, (dev, head) in enumerate(((ysame, ys4), (yother, yo4))):
             a, b = half_part(i, head, y, c)
             send(a, b, init_sem.at[i, 1 + k], dev)
@@ -126,21 +132,17 @@
     send(tok_ref, xraw.at[me4], tok_sem.at[2, 0], sib)
 
     def relay(t, d):
-        buf = bufs[t]
         if d == 0:
-            for i in ((0, 1) if t == 0 else (t + 1,)):
-                loc_w[i].wait()
-                recv(full_part(i, me4, y, 1 - c)[1], init_sem.at[i, 0], sib)
-                recv(half_part(i, me4, 1 - y, c)[1], init_sem.at[i, 1], ysame)
-                recv(half_part(i, me4, 1 - y, 1 - c)[1], init_sem.at[i, 2], yother)
-            own = buf.at[z, :, :, gx]
+            loc_w[t].wait()
+            recv(full_part(t, me4, y, 1 - c)[1], init_sem.at[t, 0], sib)
+            recv(half_part(t, me4, 1 - y, c)[1], init_sem.at[t, 1], ysame)
+            recv(half_part(t, me4, 1 - y, 1 - c)[1], init_sem.at[t, 2], yother)
+            own = unit(t, z, gx)
             send(own, own, zsem.at[t, 1, 1], zm, has_zm)
             send(own, own, zsem.at[t, 0, 1], zp, has_zp)
-            mate = buf.at[z, 1 - y, :, gx]
-            send(mate, mate, xsem.at[t, 0, 0], twin)
+            send(mates(t, gx), mates(t, gx), xsem.at[t, 0, 0], twin)
             return
-        left = buf.at[z - d, :, :, gx]
-        right = buf.at[z + d, :, :, gx]
+        left, right = unit(t, z - d, gx), unit(t, z + d, gx)
         has_l, has_r = z >= d, z + d < nz
         recv(right, zsem.at[t, 1, d], zp, has_r)
         if d + 1 < nz:
@@ -151,29 +153,35 @@
         send(right, right, xsem.at[t, 1, d], twin, has_r)
         send(left, left, xsem.at[t, 0, d], twin, has_l)
 
-    def finish(t):
-        buf = bufs[t]
-        recv(buf.at[z, 1 - y, :, 1 - gx], xsem.at[t, 0, 0], twin)
-        for d in range(1, nz):
-            recv(buf.at[z + d, :, :, 1 - gx], xsem.at[t, 1, d], twin, z + d < nz)
-            recv(buf.at[z - d, :, :, 1 - gx], xsem.at[t, 0, d], twin, z >= d)
-
-    def normalize(slot):
+    def finish(pair):
+        for t in (2 * pair, 2 * pair + 1):
+            recv(mates(t, 1 - gx), xsem.at[t, 0, 0], twin)
+            for d in range(1, nz):
+                recv(unit(t, z + d, 1 - gx), xsem.at[t, 1, d], twin, z + d < nz)
+                recv(unit(t, z - d, 1 - gx), xsem.at[t, 0, d], twin, z >= d)
+
+    def normalize(slot, first=0, count=None):
         step = 16
+        count = rows if count is None else count
 
         def body(i, _):
-            r = pl.ds(pl.multiple_of(i * step, step), step)
+            r = pl.ds(pl.multiple_of(first + i * step, step), step)
             wide = xraw[slot, r, :].astype(jnp.float32)
             inv = lax.rsqrt(jnp.mean(wide * wide, axis=-1, keepdims=True) + 1e-05)
             xn[slot, r, :] = (wide * inv * gain_ref[...]).astype(jnp.bfloat16)
             return 0
 
-        lax.fori_loop(0, rows // step, body, 0)
+        lax.fori_loop(0, count // step, body, 0)
 
     def forward_tokens(j):
         r = slice(j * prow, (j + 1) * prow)
         recv(xraw.at[ys4, r], tok_sem.at[0, j], ysame)
         send(xraw.at[ys4, r], xraw.at[ys4, r], tok_sem.at[1, j], sib)
+        normalize(ys4, j * prow, prow)
+
+    def other_tokens(j):
+        recv(xraw.at[yo4, j * prow:(j + 1) * prow], tok_sem.at[1, j], sib)
+        normalize(yo4, j * prow, prow)
 
     def project_kv(yy):
         def body(ci, _):
@@ -183,16 +191,17 @@
 
         lax.fori_loop(0, 2, body, 0)
 
-    def project_q(t):
+    def project_q(t, yy):
         buf = bufs[t]
 
         def body(i, _):
+            i = 2 * yy + i
             r = jnp.dot(xn[i], buf[...].reshape(width, SW), preferred_element_type=jnp.float32).astype(jnp.bfloat16)
             qbuf[2 * (t - 1), i] = r[:, 0:HD]
             qbuf[2 * (t - 1) + 1, i] = r[:, HD:SW]
             return 0
 
-        lax.fori_loop(0, 4, body, 0)
+        lax.fori_loop(0, 2, body, 0)
 
     def halo_send(yy, which):
         for slot in range(4):
@@ -254,47 +263,45 @@
             attend(slot, t)
             src = obuf.at[t, slot]
             if dev is None:
-                out_local.append(local(src, out_cols(me4, t), 6 + t))
+                out_local.append(local(src, out_cols(me4, t), SETS + 2 + t))
             else:
                 send(src, out_cols(me4, t), out_sem.at[t, i], dev)
 
-    relay(0, 0)
-    loc_x.wait()
-    normalize(me4)
-    relay(1, 0)
-    relay(0, 1)
+    for t in range(SETS):
+        relay(t, 0)
+        if t == 2:
+            loc_x.wait()
+            normalize(me4)
     ids_send()
-    recv(xraw.at[sib4], tok_sem.at[2, 0], sib)
-    normalize(sib4)
-    last = nz - 1 + SETS - 1
-    for w in range(2, last + 1):
+    for d in range(1, nz):
         for t in range(SETS):
-            d = w - t
-            if 0 <= d < nz:
-                relay(t, d)
-        if w == last - 2:
+            relay(t, d)
+        if d == 1:
+            recv(xraw.at[sib4], tok_sem.at[2, 0], sib)
+            normalize(sib4)
             forward_tokens(0)
-        if w == last - 1:
+        if d == max(2, nz - 2):
             forward_tokens(1)
-            finish(0)
-            project_kv(y)
-            halo_send(y, 0)
-    for j in range(2, PIECES):
-        forward_tokens(j)
-    for j in range(PIECES):
-        r = slice(j * prow, (j + 1) * prow)
-        recv(xraw.at[yo4, r], tok_sem.at[1, j], sib)
-    normalize(ys4)
-    normalize(yo4)
+            other_tokens(0)
+    finish(0)
+    project_kv(y)
+    halo_send(y, 0)
+    forward_tokens(2)
+    other_tokens(1)
+    other_tokens(2)
+    forward_tokens(3)
+    other_tokens(3)
     project_kv(1 - y)
     halo_send(1 - y, 1)
     finish(1)
-    project_q(1)
+    project_q(1, y)
+    project_q(1, 1 - y)
     ids_recv()
     halo_recv()
     attend_set(0)
     finish(2)
-    project_q(2)
+    project_q(2, y)
+    project_q(2, 1 - y)
     attend_set(1)
     for t in range(2):
         for i, (dev, head) in enumerate(((yother, yo4), (ysame, ys4), (sib, sib4))):
@@ -316,7 +323,7 @@
         ids = jnp.broadcast_to(ids[None, :], (8, rows))
         anywhere = pl.BlockSpec(memory_space=pl.ANY)
         vmem = pl.BlockSpec(memory_space=pltpu.VMEM)
-        n_send = SETS * (4 * nz) + 12 + 3 + 2 * PIECES + 1 + 2 + 12 + 6 + 2
+        n_send = SETS * (4 * nz) + 3 * SETS + 3 + 2 * PIECES + 1 + 2 + 12 + 6 + 2
         bf = jnp.bfloat16
         dma = pltpu.SemaphoreType.DMA
         half = w_query.shape[0] // 2
@@ -335,7 +342,7 @@
                 pltpu.VMEM((SLOTS, rows, SW), bf),
                 pltpu.VMEM((SLOTS, 8, rows), jnp.int32),
                 pltpu.VMEM((2, 4, rows, SW), bf),
-                dma((n_send,)), dma((8,)), dma((4, 3)), dma((SETS, 2, nz)), dma((SETS, 2, nz)),
+                dma((n_send,)), dma((SETS + 4,)), dma((SETS, 3)), dma((SETS, 2, nz)), dma((SETS, 2, nz)),
                 dma((3, PIECES)), dma((5,)), dma((2, REACH)), dma((2, 3)),
             ],
             compiler_params=pltpu.CompilerParams(

time: 112 us -> 109 us (0.973)
  Pallas kernels: 108 us -> 105 us
    pallas_call x1, Pallas kernels: 108 us -> 105 us  [on_device(): pl.pallas_call(functools.partial(kernel, n_chips), out_shape=jax.ShapeDty...]
where the time goes in v3:
time: 109 us; the launch traced here: 108 us
  Pallas kernels  105 us (96%)
  local copies, waits for them, and re-layouts  2.98 us (3%)
    pallas_call x1, Pallas kernels, on_device(): pl.pallas_call(functools.partial(kernel, n_chips), out_shape=jax.ShapeDty...  105 us
    unnamed x1, local copies, waits for them, and re-layouts  2.3 us

profile of v3, /device:TPU:9, one launch (start us, length us, event | category | flops | bytes accessed | tf_op | source)
XLA Modules:
  0.0 108.2 jit_solution(9698167714141727629)
XLA Ops:
  0.0 0.7 broadcast_add_fusion
  0.7 0.1 broadcast_bitcast_fusion
  0.7 0.6 broadcast_in_dim.16.id_ref
  1.3 104.6 %shard_map.64 = bf16[256,2048]{1,0:T(8,128)(2,1)} custom-call(bf16[256,4096]{1,0:T(8,128)(2,1)} %tok_ref.1, f32[1,4096]{1,0:T(1,128)} %bitcast.9, bf16[2,128,2048]{2,1,0:T(8,128)(2,1)} %bitcast.6, bf16[2,128,512]{2,1,0:T(8,128)(2,1)} %bitcast.7, bf16[2,128,512]{2,1,0:T(8,128)(2,1)} %bitcast.8, s32[8,256]{1,0:T(8,128)} %broadcast_in_dim.16.id_ref), custom_call_target="tpu_custom_call" | custom-call | tf_op jit(solution)/shard_map/pallas_call | solution.py:332
  105.9 2.3 %copy.8 = bf16[256,2048]{1,0:T(8,128)(2,1)} copy(bf16[256,2048]{1,0:T(8,128)(2,1)} %shard_map.64) | data formatting | bytes 2097152
